TPU v7x, 32 devices: a whole 2x2x4 slice. The times are simulated.
32 devices in a mesh: rep: 8 (over y, x, core), shard: 4 (over z).
Axes of the slice: x: 2, y: 2, z: 4, core: 2. Of those that a mesh axis runs over, the one named last changes fastest.
Arguments:
- tokens: bfloat16 [16384, 1536], P(('rep', 'shard')), may hold values from -6 to 6
- cotangent: bfloat16 [16384, 1536], P(('rep', 'shard')), may hold values from -6 to 6
- norm_first: bfloat16 [1536], P('shard'), may hold values from 0.5 to 1.5
- branch_weight: bfloat16 [1536, 2048], P(None, 'shard'), may hold values from -0.15625 to 0.15625
- gelu_weight: bfloat16 [1536, 2048], P(None, 'shard'), may hold values from -0.15625 to 0.15625
- conv_weight: bfloat16 [4, 2048], P(None, 'shard'), may hold values from -2.5 to 2.5
- conv_bias: bfloat16 [2048], P('shard'), may hold values from -2.5 to 2.5
- gate_weight: bfloat16 [16, 128, 256], P('shard'), may hold values from -0.5 to 0.5
- gate_bias: bfloat16 [16, 256], P('shard'), may hold values from -2.5 to 2.5
- decay_param: bfloat16 [2048], P('shard'), may hold values from 2.1875 to 6.875
- merge_weight: bfloat16 [2048, 1536], P('shard'), may hold values from -0.375 to 0.375
- norm_second: bfloat16 [1536], P('shard'), may hold values from 0.5 to 1.5
- feed_gate: bfloat16 [1536, 4608], P(None, 'shard'), may hold values from -0.15625 to 0.15625
- feed_up: bfloat16 [1536, 4608], P(None, 'shard'), may hold values from -0.15625 to 0.15625
- feed_down: bfloat16 [4608, 1536], P('shard'), may hold values from -0.1875 to 0.1875
- down_branch: bfloat16 [1536, 128], P(None, 'shard'), may hold values from -0.15625 to 0.15625
- up_branch: bfloat16 [128, 2048], P('shard'), may hold values from -0.75 to 0.75
- down_gelu: bfloat16 [1536, 128], P(None, 'shard'), may hold values from -0.15625 to 0.15625
- up_gelu: bfloat16 [128, 2048], P('shard'), may hold values from -0.75 to 0.75
- down_gates: bfloat16 [2048, 128], P(None, 'shard'), may hold values from -0.125 to 0.125
- up_gates: bfloat16 [128, 4096], P('shard'), may hold values from -0.75 to 0.75
- down_merge: bfloat16 [2048, 128], P(None, 'shard'), may hold values from -0.125 to 0.125
- up_merge: bfloat16 [128, 1536], P('shard'), may hold values from -0.75 to 0.75
- down_feed_gate: bfloat16 [1536, 128], P(None, 'shard'), may hold values from -0.15625 to 0.15625
- up_feed_gate: bfloat16 [128, 4608], P('shard'), may hold values from -0.75 to 0.75
- down_feed_up: bfloat16 [1536, 128], P(None, 'shard'), may hold values from -0.15625 to 0.15625
- up_feed_up: bfloat16 [128, 4608], P('shard'), may hold values from -0.75 to 0.75
- down_feed_down: bfloat16 [4608, 128], P(None, 'shard'), may hold values from -0.09375 to 0.09375
- up_feed_down: bfloat16 [128, 1536], P('shard'), may hold values from -0.75 to 0.75
- seq_lengths: int32 [32, 4], P(('rep', 'shard')), may hold values from 1 to 256, 384 in all within a row
- adapter_index: int32 [32, 4], P(('rep', 'shard')), may hold values from 0 to 7
- deal_order: int32 [8, 2048], P('rep'), may hold values from 0 to 2047, as said below
Outputs:
- layer_out: float32 [16384, 1536], P(('rep', 'shard'))
- grad_tokens: float32 [16384, 1536], P(('rep', 'shard'))
- grad_down_branch: float32 [1536, 128], P(None, 'shard')
- grad_up_branch: float32 [128, 2048], P('shard')
- grad_down_gelu: float32 [1536, 128], P(None, 'shard')
- grad_up_gelu: float32 [128, 2048], P('shard')
- grad_down_gates: float32 [2048, 128], P(None, 'shard')
- grad_up_gates: float32 [128, 4096], P('shard')
- grad_down_merge: float32 [2048, 128], P(None, 'shard')
- grad_up_merge: float32 [128, 1536], P('shard')
- grad_down_feed_gate: float32 [1536, 128], P(None, 'shard')
- grad_up_feed_gate: float32 [128, 4608], P('shard')
- grad_down_feed_up: float32 [1536, 128], P(None, 'shard')
- grad_up_feed_up: float32 [128, 4608], P('shard')
- grad_down_feed_down: float32 [4608, 128], P(None, 'shard')
- grad_up_feed_down: float32 [128, 1536], P('shard')
Inputs may be any that keep to these rules, and one draw needn't show every extreme that they name: Each row of deal_order is a permutation of 0 to 2047. Exactly 128 of the arrival rows of one device (rows b * 512 to b * 512 + 511 of its group) fill slots of each block of its group. `seq_lengths`: in every block the lengths sum to 384 and the longest is 256.
All inputs are finite; a program needn't handle non-finite values.
Results may differ from a plain program's by a relative error of at most 0.015.
Values may be sent and summed in bfloat16 or wider, within the bound.
A program may use at most 320 MiB of HBM per device.

v0:
```python
import jax
import jax.numpy as jnp
from jax import lax
from jax.sharding import PartitionSpec as P

H = 16
DH = 128
NA = 8
R = 16
NORM_EPSILON = 1e-06
DECAY_SCALE = 8.0


def matmul(left, right):
    return jnp.dot(left, right, preferred_element_type=jnp.float32)


def matmul_right_t(left, right):
    return lax.dot_general(
        left, right, (((1,), (1,)), ((), ())), preferred_element_type=jnp.float32
    )


def matmul_left_t(left, right):
    return lax.dot_general(
        left, right, (((0,), (0,)), ((), ())), preferred_element_type=jnp.float32
    )


def root_norm(values, gain):
    return (
        values * lax.rsqrt(jnp.mean(values * values, axis=-1, keepdims=True) + NORM_EPSILON) * gain
    )


def layout(lengths_row, index_row, slots_count):
    seq_count = lengths_row.shape[0]
    ends = jnp.cumsum(lengths_row)
    starts = ends - lengths_row
    slots = jnp.arange(slots_count, dtype=jnp.int32)
    segment = jnp.sum((slots[:, None] >= ends[None, :]).astype(jnp.int32), axis=1)
    start_all = jnp.concatenate([starts, ends[-1:]])
    member = segment[:, None] == jnp.arange(seq_count + 1, dtype=jnp.int32)[None, :]
    position = slots - jnp.sum(jnp.where(member, start_all[None, :], 0), axis=1)
    live_rows = segment < seq_count
    chosen = jnp.sum(jnp.where(member[:, :seq_count], index_row[None, :], 0), axis=1)
    adapter_hit = (chosen[:, None] == jnp.arange(NA, dtype=jnp.int32)[None, :]) & live_rows[:, None]
    adapter_mask = jnp.repeat(adapter_hit.astype(jnp.float32), R, axis=1)
    return (position, live_rows.astype(jnp.float32), adapter_mask)


def conv_apply(values, weight, bias, position):
    total = bias[None, :] + weight[0][None, :] * values
    for offset in range(1, weight.shape[0]):
        moved = jnp.concatenate(
            [jnp.zeros((offset, values.shape[1]), values.dtype), values[:-offset]], axis=0
        )
        keeper = (position >= offset).astype(values.dtype)[:, None]
        total = total + weight[offset][None, :] * moved * keeper
    return total


def combine(earlier, later):
    return (earlier[0] * later[0], later[0] * earlier[1] + later[1])


def recurrence(gate_logits, conv_out, gelu_in, decay, position):
    rows_count = conv_out.shape[0]
    shaped = gate_logits.reshape(rows_count, H, 2 * DH)
    input_gate = jax.nn.sigmoid(shaped[:, :, :DH]).reshape(rows_count, H * DH)
    rec_gate = jax.nn.sigmoid(shaped[:, :, DH:]).reshape(rows_count, H * DH)
    log_decay = -DECAY_SCALE * rec_gate * jax.nn.softplus(-decay)[None, :]
    decay_now = jnp.exp(log_decay)
    first = (position == 0)[:, None]
    scale_in = jnp.where(first, 1.0, jnp.sqrt(-jnp.expm1(2.0 * log_decay)))
    carried = jnp.where(first, 0.0, decay_now)
    driven = scale_in * input_gate * conv_out
    unused, state = lax.associative_scan(combine, (carried, driven), axis=0)
    return state * jax.nn.gelu(gelu_in)


def feed_mix(hidden_gate, hidden_up):
    return jax.nn.gelu(hidden_gate) * hidden_up


def local(
    tokens,
    cotangent,
    norm_first,
    branch_weight,
    gelu_weight,
    conv_weight,
    conv_bias,
    gate_weight,
    gate_bias,
    decay_param,
    merge_weight,
    norm_second,
    feed_gate,
    feed_up,
    feed_down,
    down_branch,
    up_branch,
    down_gelu,
    up_gelu,
    down_gates,
    up_gates,
    down_merge,
    up_merge,
    down_feed_gate,
    up_feed_gate,
    down_feed_up,
    up_feed_up,
    down_feed_down,
    up_feed_down,
    seq_lengths,
    adapter_index,
    deal_order,
):
    rows_here = tokens.shape[0]
    shards = lax.axis_size("shard")
    my_index = lax.axis_index("shard")
    deal_row = deal_order[0]
    group_rows = deal_row.shape[0]
    gathered = (
        lax.all_gather(tokens, "shard", axis=0, tiled=True),
        lax.all_gather(cotangent, "shard", axis=0, tiled=True),
    )
    my_picks = lax.dynamic_slice_in_dim(deal_row, my_index * rows_here, rows_here)
    work_in = jnp.take(gathered[0], my_picks, axis=0)
    work_cot = jnp.take(gathered[1], my_picks, axis=0)
    block_parts = (
        lax.all_gather(norm_first, "shard", axis=0, tiled=True),
        lax.all_gather(branch_weight, "shard", axis=1, tiled=True),
        lax.all_gather(gelu_weight, "shard", axis=1, tiled=True),
        lax.all_gather(conv_weight, "shard", axis=1, tiled=True),
        lax.all_gather(conv_bias, "shard", axis=0, tiled=True),
        lax.all_gather(gate_weight, "shard", axis=0, tiled=True),
        lax.all_gather(gate_bias, "shard", axis=0, tiled=True),
        lax.all_gather(decay_param, "shard", axis=0, tiled=True),
        lax.all_gather(merge_weight, "shard", axis=0, tiled=True),
    )
    (
        gain_first,
        weight_branch,
        weight_gelu,
        taps_conv,
        bias_conv,
        weight_gates,
        bias_gates,
        decay_all,
        weight_merge,
    ) = block_parts
    adapter_parts = (
        lax.all_gather(down_branch, "shard", axis=1, tiled=True),
        lax.all_gather(up_branch, "shard", axis=0, tiled=True),
        lax.all_gather(down_gelu, "shard", axis=1, tiled=True),
        lax.all_gather(up_gelu, "shard", axis=0, tiled=True),
        lax.all_gather(down_gates, "shard", axis=1, tiled=True),
        lax.all_gather(up_gates, "shard", axis=0, tiled=True),
        lax.all_gather(down_merge, "shard", axis=1, tiled=True),
        lax.all_gather(up_merge, "shard", axis=0, tiled=True),
        lax.all_gather(down_feed_gate, "shard", axis=1, tiled=True),
        lax.all_gather(up_feed_gate, "shard", axis=0, tiled=True),
        lax.all_gather(down_feed_up, "shard", axis=1, tiled=True),
        lax.all_gather(up_feed_up, "shard", axis=0, tiled=True),
        lax.all_gather(down_feed_down, "shard", axis=1, tiled=True),
        lax.all_gather(up_feed_down, "shard", axis=0, tiled=True),
    )
    (
        fact_down_branch,
        fact_up_branch,
        fact_down_gelu,
        fact_up_gelu,
        fact_down_gates,
        fact_up_gates,
        fact_down_merge,
        fact_up_merge,
        fact_down_fgate,
        fact_up_fgate,
        fact_down_fup,
        fact_up_fup,
        fact_down_fdown,
        fact_up_fdown,
    ) = adapter_parts
    position, live_rows, adapter_mask = layout(seq_lengths[0], adapter_index[0], rows_here)

    def adapter_forward(act, down, up):
        rank_part = (matmul(act, down) * adapter_mask).astype(jnp.bfloat16)
        return (rank_part, matmul(rank_part, up))

    def adapter_backward(grad_low, act, rank_part, up):
        grad_rank = (matmul_right_t(grad_low, up) * adapter_mask).astype(jnp.bfloat16)
        return (grad_rank, matmul_left_t(act, grad_rank), matmul_left_t(rank_part, grad_low))

    gain_first_f = gain_first.astype(jnp.float32)
    rows_in = work_in.astype(jnp.float32)
    normed_first, first_pull = jax.vjp(lambda values: root_norm(values, gain_first_f), rows_in)
    act_first = normed_first.astype(jnp.bfloat16)
    rank_branch, extra_branch = adapter_forward(act_first, fact_down_branch, fact_up_branch)
    branch = matmul(act_first, weight_branch) + extra_branch
    rank_gelu, extra_gelu = adapter_forward(act_first, fact_down_gelu, fact_up_gelu)
    gelu_in = matmul(act_first, weight_gelu) + extra_gelu
    taps_f = taps_conv.astype(jnp.float32)
    bias_f = bias_conv.astype(jnp.float32)
    conv_out, conv_pull = jax.vjp(
        lambda values: conv_apply(values, taps_f, bias_f, position), branch
    )
    conv_low = conv_out.astype(jnp.bfloat16)
    heads = conv_low.reshape(rows_here, H, DH)
    blockwise = jnp.einsum(
        "thd,hde->the", heads, weight_gates, preferred_element_type=jnp.float32
    ).reshape(rows_here, 2 * H * DH)
    rank_gates, extra_gates = adapter_forward(conv_low, fact_down_gates, fact_up_gates)
    gate_logits = blockwise + bias_gates.astype(jnp.float32).reshape(-1)[None, :] + extra_gates
    decay_f = decay_all.astype(jnp.float32)
    mixed, mixed_pull = jax.vjp(
        lambda logits, conv_in, gelu_part: recurrence(
            logits, conv_in, gelu_part, decay_f, position
        ),
        gate_logits,
        conv_out,
        gelu_in,
    )
    mixed_low = mixed.astype(jnp.bfloat16)
    rank_merge, extra_merge = adapter_forward(mixed_low, fact_down_merge, fact_up_merge)
    resid = rows_in + matmul(mixed_low, weight_merge) + extra_merge
    feed_parts = (
        lax.all_gather(norm_second, "shard", axis=0, tiled=True),
        lax.all_gather(feed_gate, "shard", axis=1, tiled=True),
        lax.all_gather(feed_up, "shard", axis=1, tiled=True),
        lax.all_gather(feed_down, "shard", axis=0, tiled=True),
    )
    gain_second, weight_fgate, weight_fup, weight_fdown = feed_parts
    gain_second_f = gain_second.astype(jnp.float32)
    normed_second, second_pull = jax.vjp(lambda values: root_norm(values, gain_second_f), resid)
    act_second = normed_second.astype(jnp.bfloat16)
    rank_fgate, extra_fgate = adapter_forward(act_second, fact_down_fgate, fact_up_fgate)
    hidden_gate = matmul(act_second, weight_fgate) + extra_fgate
    rank_fup, extra_fup = adapter_forward(act_second, fact_down_fup, fact_up_fup)
    hidden_up = matmul(act_second, weight_fup) + extra_fup
    hidden, hidden_pull = jax.vjp(feed_mix, hidden_gate, hidden_up)
    hidden_low = hidden.astype(jnp.bfloat16)
    rank_fdown, extra_fdown = adapter_forward(hidden_low, fact_down_fdown, fact_up_fdown)
    work_out = (resid + matmul(hidden_low, weight_fdown) + extra_fdown) * live_rows[:, None]
    grad_out = work_cot.astype(jnp.float32) * live_rows[:, None]
    grad_out_low = grad_out.astype(jnp.bfloat16)
    grad_rank_fdown, grad_down_fdown, grad_up_fdown = adapter_backward(
        grad_out_low, hidden_low, rank_fdown, fact_up_fdown
    )
    grad_hidden = matmul_right_t(grad_out_low, weight_fdown) + matmul_right_t(
        grad_rank_fdown, fact_down_fdown
    )
    grad_hgate, grad_hup = hidden_pull(grad_hidden)
    grad_hgate_low = grad_hgate.astype(jnp.bfloat16)
    grad_hup_low = grad_hup.astype(jnp.bfloat16)
    grad_rank_fgate, grad_down_fgate, grad_up_fgate = adapter_backward(
        grad_hgate_low, act_second, rank_fgate, fact_up_fgate
    )
    grad_rank_fup, grad_down_fup, grad_up_fup = adapter_backward(
        grad_hup_low, act_second, rank_fup, fact_up_fup
    )
    grad_second = (
        matmul_right_t(grad_hgate_low, weight_fgate)
        + matmul_right_t(grad_hup_low, weight_fup)
        + matmul_right_t(grad_rank_fgate, fact_down_fgate)
        + matmul_right_t(grad_rank_fup, fact_down_fup)
    )
    grad_resid = grad_out + second_pull(grad_second)[0]
    grad_resid_low = grad_resid.astype(jnp.bfloat16)
    grad_rank_merge, grad_down_merge, grad_up_merge = adapter_backward(
        grad_resid_low, mixed_low, rank_merge, fact_up_merge
    )
    grad_mixed = matmul_right_t(grad_resid_low, weight_merge) + matmul_right_t(
        grad_rank_merge, fact_down_merge
    )
    grad_logits, grad_conv_direct, grad_gelu_in = mixed_pull(grad_mixed)
    grad_logits_low = grad_logits.astype(jnp.bfloat16)
    grad_rank_gates, grad_down_gates, grad_up_gates = adapter_backward(
        grad_logits_low, conv_low, rank_gates, fact_up_gates
    )
    grad_heads = jnp.einsum(
        "the,hde->thd",
        grad_logits_low.reshape(rows_here, H, 2 * DH),
        weight_gates,
        preferred_element_type=jnp.float32,
    ).reshape(rows_here, H * DH)
    grad_conv = grad_conv_direct + grad_heads + matmul_right_t(grad_rank_gates, fact_down_gates)
    grad_branch = conv_pull(grad_conv)[0]
    grad_branch_low = grad_branch.astype(jnp.bfloat16)
    grad_gelu_low = grad_gelu_in.astype(jnp.bfloat16)
    grad_rank_branch, grad_down_branch, grad_up_branch = adapter_backward(
        grad_branch_low, act_first, rank_branch, fact_up_branch
    )
    grad_rank_gelu, grad_down_gelu, grad_up_gelu = adapter_backward(
        grad_gelu_low, act_first, rank_gelu, fact_up_gelu
    )
    grad_first = (
        matmul_right_t(grad_branch_low, weight_branch)
        + matmul_right_t(grad_gelu_low, weight_gelu)
        + matmul_right_t(grad_rank_branch, fact_down_branch)
        + matmul_right_t(grad_rank_gelu, fact_down_gelu)
    )
    grad_work = grad_resid + first_pull(grad_first)[0]
    collected = (
        lax.all_gather(work_out, "shard", axis=0, tiled=True),
        lax.all_gather(grad_work, "shard", axis=0, tiled=True),
    )
    inverse = (
        jnp.zeros((group_rows,), jnp.int32)
        .at[deal_row]
        .set(jnp.arange(group_rows, dtype=jnp.int32))
    )
    my_rows = lax.dynamic_slice_in_dim(inverse, my_index * rows_here, rows_here)
    layer_out = jnp.take(collected[0], my_rows, axis=0)
    grad_tokens = jnp.take(collected[1], my_rows, axis=0)
    part_width = grad_down_branch.shape[1] // shards
    summed = lax.psum(
        (
            grad_down_branch,
            grad_up_branch,
            grad_down_gelu,
            grad_up_gelu,
            grad_down_gates,
            grad_up_gates,
            grad_down_merge,
            grad_up_merge,
            grad_down_fgate,
            grad_up_fgate,
            grad_down_fup,
            grad_up_fup,
            grad_down_fdown,
            grad_up_fdown,
        ),
        ("rep", "shard"),
    )
    owned = tuple(
        (
            lax.dynamic_slice_in_dim(
                summed[number], my_index * part_width, part_width, 1 - number % 2
            )
            for number in range(14)
        )
    )
    return (
        layer_out,
        grad_tokens,
        owned[0],
        owned[1],
        owned[2],
        owned[3],
        owned[4],
        owned[5],
        owned[6],
        owned[7],
        owned[8],
        owned[9],
        owned[10],
        owned[11],
        owned[12],
        owned[13],
    )


def solution(mesh):
    in_specs = (
        P(("rep", "shard"), None),
        P(("rep", "shard"), None),
        P("shard"),
        P(None, "shard"),
        P(None, "shard"),
        P(None, "shard"),
        P("shard"),
        P("shard", None, None),
        P("shard", None),
        P("shard"),
        P("shard", None),
        P("shard"),
        P(None, "shard"),
        P(None, "shard"),
        P("shard", None),
        P(None, "shard"),
        P("shard", None),
        P(None, "shard"),
        P("shard", None),
        P(None, "shard"),
        P("shard", None),
        P(None, "shard"),
        P("shard", None),
        P(None, "shard"),
        P("shard", None),
        P(None, "shard"),
        P("shard", None),
        P(None, "shard"),
        P("shard", None),
        P(("rep", "shard"), None),
        P(("rep", "shard"), None),
        P("rep", None),
    )
    out_specs = (
        P(("rep", "shard"), None),
        P(("rep", "shard"), None),
        P(None, "shard"),
        P("shard", None),
        P(None, "shard"),
        P("shard", None),
        P(None, "shard"),
        P("shard", None),
        P(None, "shard"),
        P("shard", None),
        P(None, "shard"),
        P("shard", None),
        P(None, "shard"),
        P("shard", None),
        P(None, "shard"),
        P("shard", None),
    )
    return jax.shard_map(local, mesh=mesh, in_specs=in_specs, out_specs=out_specs, check_vma=False)
```

profile of v0, /device:TPU:0, one launch (start us, length us, event | category | flops | bytes accessed | tf_op | source)
XLA Modules:
  0.0 3010.1 jit_solution(17063541124897532782)
XLA Ops:
  19.0 15.6 all-gather.1
  35.0 17.7 all_gather.98
  52.7 23.4 all_gather.99
  76.9 16.7 all_gather.95
  93.6 14.6 all-gather
  108.3 20.1 all_gather.102
  128.4 15.4 all-gather.2
  143.8 12.0 all-gather.3
  156.5 17.4 all_gather.106
  173.8 23.5 all_gather.107
  197.3 24.9 all_gather.109
  222.2 22.7 all_gather.110
  244.9 12.1 all-gather.4
  257.6 20.9 all_gather.116
  278.5 22.2 all_gather.113
  300.7 15.2 all_gather.120
  347.6 8.9 copy.113
  362.9 8.3 add_add_fusion
  371.1 9.3 copy.142
  398.1 11.7 exponential_select_fusion
  409.8 9.8 slice.325
  419.6 9.8 slice.326
  429.5 9.8 slice.324
  439.3 9.8 slice.328
  556.3 10.1 slice.323
  566.5 10.1 slice.388
  598.7 8.7 pad.364
  616.3 16.5 pad.367
  638.7 16.5 pad.366
  678.3 31.0 %all-gather.47.cloned.1.call-done = bf16[2048,1536]{1,0:T(8,128)(2,1)} async-done(((bf16[512,1536]{1,0:T(8,128)(2,1)}), bf16[2048,1536]{1,0:T(8,128)(2,1)}) %all-gather.47.cloned.1.call-update) | async-done | bytes 6291472 | tf_op jit(solution)/shard_map/all_gather | solution.py:127
  709.3 8.2 gather_fusion.2
  720.0 233.1 %all-gather.37.cloned.1.call-done = bf16[1536,4608]{1,0:T(8,128)(2,1)} async-done(((bf16[1536,1152]{1,0:T(8,128)(2,1)}), bf16[1536,4608]{1,0:T(8,128)(2,1)}) %all-gather.37.cloned.1.call-update) | async-done | bytes 14155792 | tf_op jit(solution)/shard_map/all_gather | solution.py:231
  953.1 12.9 fusion.130
  965.9 230.9 %all-gather.33.cloned.1.call-done = bf16[1536,4608]{1,0:T(8,128)(2,1)} async-done(((bf16[1536,1152]{1,0:T(8,128)(2,1)}), bf16[1536,4608]{1,0:T(8,128)(2,1)}) %all-gather.33.cloned.1.call-update) | async-done | bytes 14155792 | tf_op jit(solution)/shard_map/all_gather | solution.py:230
  1196.8 12.8 fusion.129
  1209.7 17.2 all-gather.39.cloned.1.call-done
  1226.9 9.0 convolution_add_fusion.1
  1235.9 22.2 all-gather.35.cloned.1.call-done
  1258.1 10.0 convolution_add_fusion.2
  1268.1 234.5 %all-gather.41.cloned.1.call-done = bf16[4608,1536]{1,0:T(8,128)(2,1)} async-done(((bf16[1152,1536]{1,0:T(8,128)(2,1)}), bf16[4608,1536]{1,0:T(8,128)(2,1)}) %all-gather.41.cloned.1.call-update) | async-done | bytes 14155792 | tf_op jit(solution)/shard_map/all_gather | solution.py:232
  1502.6 13.4 fusion.95
  1516.0 16.8 all-gather.43.cloned.1.call-done
  1532.8 17.3 multiply_convert_fusion
  1550.1 13.4 fusion.131
  1564.9 10.3 convolution_add_fusion.12
  1598.4 9.8 slice.389
  1615.1 9.8 slice.390
  1714.0 8.8 pad.425
  1727.5 8.6 pad.450
  1736.2 8.7 pad.375
  1749.8 11.2 multiply_add_fusion.1
  1763.9 16.6 pad.426
  1780.5 16.5 pad.427
  1797.0 16.6 pad.451
  1813.6 16.6 pad.452
  1830.2 16.9 pad.370
  1847.1 16.9 pad.428
  1864.0 18.5 multiply_multiply_fusion.5
  1977.3 12.4 convolution_add_fusion.13
  2019.8 528.0 %all-reduce.96.cloned.1.call-done = (f32[1536,128]{0,1:T(8,128)}, f32[128,2048]{1,0:T(8,128)}, f32[1536,128]{0,1:T(8,128)}, f32[128,2048]{1,0:T(8,128)}, f32[204...) async-done(((f32[1536,128]{0,1:T(8,128)}, ...) | async-done | bytes 18087952 | tf_op jit(solution)/shard_map/psum | solution.py:318
  2563.3 207.1 %all-gather.45.cloned.1.call-done = f32[2048,1536]{1,0:T(8,128)} async-done(((f32[512,1536]{1,0:T(8,128)}), f32[2048,1536]{1,0:T(8,128)}) %all-gather.45.cloned.1.call-update) | async-done | bytes 12582928 | tf_op jit(solution)/shard_map/all_gather | solution.py:306
  2770.3 8.3 gather_fusion.1
  2778.6 210.2 %all-gather.49.cloned.1.call-done = f32[2048,1536]{1,0:T(8,128)} async-done(((f32[512,1536]{1,0:T(8,128)}), f32[2048,1536]{1,0:T(8,128)}) %all-gather.49.cloned.1.call-update) | async-done | bytes 12582928 | tf_op jit(solution)/shard_map/all_gather | solution.py:307
  2988.8 9.1 gather_fusion.3
  (797 shorter events, 515.4 us)
Async XLA Ops:
  7.2 310.7 %all-gather.21.cloned.1.call-start = ((), (), s32[]{:S(2)}) async-start(), calls=%async_computation | async-start | bytes 7864320 | tf_op jit(solution)/shard_map/all_gather | solution.py:126
  7.9 321.1 %all-gather.23.cloned.1.call-start = ((), (), s32[]{:S(2)}) async-start(), calls=%async_computation.1 | async-start | bytes 7864320 | tf_op jit(solution)/shard_map/all_gather | solution.py:134
  8.7 332.4 %all-gather.25.cloned.1.call-start = ((), (), s32[]{:S(2)}) async-start(), calls=%async_computation.2 | async-start | bytes 1310720 | tf_op jit(solution)/shard_map/all_gather | solution.py:138
  9.4 353.5 %all-gather.27.cloned.1.call-start = ((), (), s32[]{:S(2)}) async-start(), calls=%async_computation.3 | async-start | bytes 1310720 | tf_op jit(solution)/shard_map/all_gather | solution.py:160
  10.0 645.9 %all-gather.29.cloned.1.call-start = ((), (), s32[]{:S(2)}) async-start(), calls=%async_computation.4 | async-start | bytes 7864320 | tf_op jit(solution)/shard_map/all_gather | solution.py:135
  10.6 657.5 %all-gather.31.cloned.1.call-start = ((), (), s32[]{:S(2)}) async-start(), calls=%async_computation.5 | async-start | bytes 7864320 | tf_op jit(solution)/shard_map/all_gather | solution.py:141
  11.1 698.2 %all-gather.47.cloned.1.call-start = ((), (), s32[]{:S(2)}) async-start(), calls=%async_computation.13 | async-start | bytes 7864320 | tf_op jit(solution)/shard_map/all_gather | solution.py:127
  11.9 941.2 %all-gather.37.cloned.1.call-start = ((), (), s32[]{:S(2)}) async-start(), calls=%async_computation.8 | async-start | bytes 17694720 | tf_op jit(solution)/shard_map/all_gather | solution.py:231
  12.7 22.1 copy-start.211
  12.7 22.3 copy-start.168
  12.7 40.0 %copy-start.157 = (bf16[32,2048]{1,0:T(8,128)(2,1)S(1)}, bf16[32,2048]{1,0:T(8,128)(2,1)}, u32[]{:S(2)}) copy-start(bf16[32,2048]{1,0:T(8,128)(2,1)} %param.52) | copy-start | bytes 393220
  12.7 64.2 %copy-start.204 = (bf16[4,512]{1,0:T(4,128)(2,1)S(1)}, bf16[4,512]{1,0:T(4,128)(2,1)}, u32[]{:S(2)}) copy-start(bf16[4,512]{1,0:T(4,128)(2,1)} %param.41) | copy-start | bytes 12292
  12.7 80.9 %copy-start.206 = (bf16[512]{0:T(512)(128)(2,1)S(1)}, bf16[512]{0:T(512)(128)(2,1)}, u32[]{:S(2)}) copy-start(bf16[512]{0:T(512)(128)(2,1)} %param.42) | copy-start | bytes 3076
  12.7 1184.1 %all-gather.33.cloned.1.call-start = ((), (), s32[]{:S(2)}) async-start(), calls=%async_computation.6 | async-start | bytes 17694720 | tf_op jit(solution)/shard_map/all_gather | solution.py:230
  13.4 94.8 %copy-start.158 = (bf16[2048,32]{0,1:T(8,128)(2,1)S(1)}, bf16[2048,32]{0,1:T(8,128)(2,1)}, u32[]{:S(2)}) copy-start(bf16[2048,32]{0,1:T(8,128)(2,1)} %param.55) | copy-start | bytes 393220
  13.5 114.9 %copy-start.205 = (bf16[4,256]{1,0:T(4,128)(2,1)S(1)}, bf16[4,256]{1,0:T(4,128)(2,1)}, u32[]{:S(2)}) copy-start(bf16[4,256]{1,0:T(4,128)(2,1)} %param.44) | copy-start | bytes 6148
  13.5 130.4 %copy-start.207 = (bf16[512]{0:T(512)(128)(2,1)S(1)}, bf16[512]{0:T(512)(128)(2,1)}, u32[]{:S(2)}) copy-start(bf16[512]{0:T(512)(128)(2,1)} %param.45) | copy-start | bytes 3076
  13.5 143.0 %copy-start.169 = (bf16[1536,32]{0,1:T(8,128)(2,1)S(1)}, bf16[1536,32]{0,1:T(8,128)(2,1)}, u32[]{:S(2)}) copy-start(bf16[1536,32]{0,1:T(8,128)(2,1)} %param.53) | copy-start | bytes 294916
  13.5 160.3 %copy-start.159 = (bf16[32,2048]{1,0:T(8,128)(2,1)S(1)}, bf16[32,2048]{1,0:T(8,128)(2,1)}, u32[]{:S(2)}) copy-start(bf16[32,2048]{1,0:T(8,128)(2,1)} %param.54) | copy-start | bytes 393220
  13.5 1213.4 %all-gather.39.cloned.1.call-start = ((), (), s32[]{:S(2)}) async-start(), calls=%async_computation.9 | async-start | bytes 1474560 | tf_op jit(solution)/shard_map/all_gather | solution.py:166
  14.1 183.2 %copy-start.160 = (bf16[2048,32]{0,1:T(8,128)(2,1)S(1)}, bf16[2048,32]{0,1:T(8,128)(2,1)}, u32[]{:S(2)}) copy-start(bf16[2048,32]{0,1:T(8,128)(2,1)} %param.57) | copy-start | bytes 393220
  14.1 1244.0 %all-gather.35.cloned.1.call-start = ((), (), s32[]{:S(2)}) async-start(), calls=%async_computation.7 | async-start | bytes 1474560 | tf_op jit(solution)/shard_map/all_gather | solution.py:164
  14.8 207.3 %copy-start.170 = (bf16[32,1536]{1,0:T(8,128)(2,1)S(1)}, bf16[32,1536]{1,0:T(8,128)(2,1)}, u32[]{:S(2)}) copy-start(bf16[32,1536]{1,0:T(8,128)(2,1)} %param.58) | copy-start | bytes 294916
  14.8 230.0 %copy-start.209 = (bf16[384]{0:T(512)(128)(2,1)S(1)}, bf16[384]{0:T(512)(128)(2,1)}, u32[]{:S(2)}) copy-start(bf16[384]{0:T(512)(128)(2,1)} %param.47) | copy-start | bytes 2308
  14.9 242.7 %copy-start.171 = (bf16[1536,32]{0,1:T(8,128)(2,1)S(1)}, bf16[1536,32]{0,1:T(8,128)(2,1)}, u32[]{:S(2)}) copy-start(bf16[1536,32]{0,1:T(8,128)(2,1)} %param.61) | copy-start | bytes 294916
  14.9 263.6 %copy-start.172 = (bf16[1536,32]{0,1:T(8,128)(2,1)S(1)}, bf16[1536,32]{0,1:T(8,128)(2,1)}, u32[]{:S(2)}) copy-start(bf16[1536,32]{0,1:T(8,128)(2,1)} %param.59) | copy-start | bytes 294916
  14.9 285.8 %copy-start.173 = (bf16[32,1536]{1,0:T(8,128)(2,1)S(1)}, bf16[32,1536]{1,0:T(8,128)(2,1)}, u32[]{:S(2)}) copy-start(bf16[32,1536]{1,0:T(8,128)(2,1)} %param.64) | copy-start | bytes 294916
  14.9 1487.7 %all-gather.41.cloned.1.call-start = ((), (), s32[]{:S(2)}) async-start(), calls=%async_computation.10 | async-start | bytes 17694720 | tf_op jit(solution)/shard_map/all_gather | solution.py:232
  15.5 1517.3 %all-gather.43.cloned.1.call-start = ((), (), s32[]{:S(2)}) async-start(), calls=%async_computation.11 | async-start | bytes 1474560 | tf_op jit(solution)/shard_map/all_gather | solution.py:167
  16.2 2531.6 %all-reduce.96.cloned.1.call-start = ((), (), s32[]{:S(2)}) async-start(), calls=%async_computation.15 | async-start | bytes 36175872 | tf_op jit(solution)/shard_map/psum | solution.py:318
  34.7 291.6 %copy-start.177 = (f32[1536]{0:T(1024)}, f32[1536]{0:T(1024)S(1)}, u32[]{:S(2)}) copy-start(f32[1536]{0:T(1024)S(1)} %reshape.246) | copy-start | bytes 18436
  52.7 275.7 %copy-start.72 = (bf16[1536,128]{0,1:T(8,128)(2,1)}, bf16[1536,128]{0,1:T(8,128)(2,1)S(1)}, u32[]{:S(2)}) copy-start(bf16[1536,128]{0,1:T(8,128)(2,1)S(1)} %all_gather.98) | copy-start | bytes 1179652
  76.0 258.5 %copy-start.49 = (bf16[128,2048]{1,0:T(8,128)(2,1)}, bf16[128,2048]{1,0:T(8,128)(2,1)S(1)}, u32[]{:S(2)}) copy-start(bf16[128,2048]{1,0:T(8,128)(2,1)S(1)} %all_gather.99) | copy-start | bytes 1572868
  76.8 321.3 %copy-start.198 = (pred[512]{0:T(512)(128)(4,1)}, pred[512]{0:T(512)(128)(4,1)S(1)}, u32[]{:S(2)}) copy-start(pred[512]{0:T(512)(128)(4,1)S(1)} %get-tuple-element.146) | copy-start | bytes 1540
  93.6 241.7 %copy-start.175 = (f32[1,2048]{1,0:T(1,128)}, f32[1,2048]{1,0:T(1,128)S(1)}, u32[]{:S(2)}) copy-start(f32[1,2048]{1,0:T(1,128)S(1)} %get-tuple-element.140) | copy-start | bytes 24580
  93.6 241.7 %copy-start.179 = (f32[1,2048]{1,0:T(1,128)}, f32[1,2048]{1,0:T(1,128)S(1)}, u32[]{:S(2)}) copy-start(f32[1,2048]{1,0:T(1,128)S(1)} %get-tuple-element.141) | copy-start | bytes 24580
  93.6 241.7 %copy-start.181 = (f32[1,2048]{1,0:T(1,128)}, f32[1,2048]{1,0:T(1,128)S(1)}, u32[]{:S(2)}) copy-start(f32[1,2048]{1,0:T(1,128)S(1)} %get-tuple-element.143) | copy-start | bytes 24580
  93.6 241.7 %copy-start.183 = (f32[1,2048]{1,0:T(1,128)}, f32[1,2048]{1,0:T(1,128)S(1)}, u32[]{:S(2)}) copy-start(f32[1,2048]{1,0:T(1,128)S(1)} %get-tuple-element.142) | copy-start | bytes 24580
  128.3 228.2 %copy-start.46 = (bf16[2048,128]{0,1:T(8,128)(2,1)}, bf16[2048,128]{0,1:T(8,128)(2,1)S(1)}, u32[]{:S(2)}) copy-start(bf16[2048,128]{0,1:T(8,128)(2,1)S(1)} %all_gather.102) | copy-start | bytes 1572868
  156.5 241.7 %copy-start.151 = (f32[2048]{0:T(1024)}, f32[2048]{0:T(1024)S(1)}, u32[]{:S(2)}) copy-start(f32[2048]{0:T(1024)S(1)} %get-tuple-element.145) | copy-start | bytes 24580
  328.4 327.5 %copy-start.12 = (bf16[512,1536]{1,0:T(8,128)(2,1)}, bf16[512,1536]{1,0:T(8,128)(2,1)S(1)}, u32[]{:S(2)}) copy-start(bf16[512,1536]{1,0:T(8,128)(2,1)S(1)} %fusion.33) | copy-start | bytes 4718596
  497.8 41.8 %copy-start.62 = (f32[32,2048]{1,0:T(8,128)}, f32[32,2048]{1,0:T(8,128)S(1)}, u32[]{:S(2)}) copy-start(f32[32,2048]{1,0:T(8,128)S(1)} %slice.342) | copy-start | bytes 786436
  501.5 33.2 %copy-start.76 = (f32[64,2048]{1,0:T(8,128)S(1)}, f32[64,2048]{1,0:T(8,128)}, u32[]{:S(2)}) copy-start(f32[64,2048]{1,0:T(8,128)} %get-tuple-element.95) | copy-start | bytes 1572868
  502.6 47.3 %copy-start.111 = (f32[16,2048]{1,0:T(8,128)}, f32[16,2048]{1,0:T(8,128)S(1)}, u32[]{:S(2)}) copy-start(f32[16,2048]{1,0:T(8,128)S(1)} %slice.349) | copy-start | bytes 393220
  505.2 44.6 %copy-start.88 = (f32[16,2048]{1,0:T(8,128)}, f32[16,2048]{1,0:T(8,128)S(1)}, u32[]{:S(2)}) copy-start(f32[16,2048]{1,0:T(8,128)S(1)} %slice.348) | copy-start | bytes 393220
  506.3 43.6 %copy-start.113 = (f32[16,2048]{1,0:T(8,128)}, f32[16,2048]{1,0:T(8,128)S(1)}, u32[]{:S(2)}) copy-start(f32[16,2048]{1,0:T(8,128)S(1)} %slice.352) | copy-start | bytes 393220
  507.3 24.9 copy-start.130
  508.0 47.4 %copy-start.126 = (f32[8,2048]{1,0:T(8,128)}, f32[8,2048]{1,0:T(8,128)S(1)}, u32[]{:S(2)}) copy-start(f32[8,2048]{1,0:T(8,128)S(1)} %slice.354) | copy-start | bytes 196612
  508.1 24.1 copy-start.132
  521.7 33.7 %copy-start.162 = (f32[1,2048]{1,0:T(1,128)}, f32[1,2048]{1,0:T(1,128)S(1)}, u32[]{:S(2)}) copy-start(f32[1,2048]{1,0:T(1,128)S(1)} %get-tuple-element.138) | copy-start | bytes 24580
  528.2 50.0 %copy-start.128 = (f32[7,2048]{1,0:T(8,128)}, f32[7,2048]{1,0:T(8,128)S(1)}, u32[]{:S(2)}) copy-start(f32[7,2048]{1,0:T(8,128)S(1)} %slice.353) | copy-start | bytes 172036
  530.5 48.5 %copy-start.109 = (f32[15,2048]{1,0:T(8,128)}, f32[15,2048]{1,0:T(8,128)S(1)}, u32[]{:S(2)}) copy-start(f32[15,2048]{1,0:T(8,128)S(1)} %slice.347) | copy-start | bytes 368644
  534.8 45.7 %copy-start.77 = (f32[31,2048]{1,0:T(8,128)}, f32[31,2048]{1,0:T(8,128)S(1)}, u32[]{:S(2)}) copy-start(f32[31,2048]{1,0:T(8,128)S(1)} %slice.341) | copy-start | bytes 761860
  556.3 21.9 copy-start.190
  677.1 519.7 %copy-start.14 = (bf16[512,1536]{1,0:T(8,128)(2,1)}, bf16[512,1536]{1,0:T(8,128)(2,1)S(1)}, u32[]{:S(2)}) copy-start(bf16[512,1536]{1,0:T(8,128)(2,1)S(1)} %multiply_convert_fusion.3) | copy-start | bytes 4718596
  677.7 549.2 %copy-start.92 = (bf16[512,128]{1,0:T(8,128)(2,1)}, bf16[512,128]{1,0:T(8,128)(2,1)S(1)}, u32[]{:S(2)}) copy-start(bf16[512,128]{1,0:T(8,128)(2,1)S(1)} %fusion.49) | copy-start | bytes 393220
  678.3 579.7 %copy-start.94 = (bf16[512,128]{1,0:T(8,128)(2,1)}, bf16[512,128]{1,0:T(8,128)(2,1)S(1)}, u32[]{:S(2)}) copy-start(bf16[512,128]{1,0:T(8,128)(2,1)S(1)} %fusion.48) | copy-start | bytes 393220
  720.0 812.8 %copy-start.155 = (bf16[512,128]{1,0:T(8,128)(2,1)}, bf16[512,128]{1,0:T(8,128)(2,1)S(1)}, u32[]{:S(2)}) copy-start(bf16[512,128]{1,0:T(8,128)(2,1)S(1)} %fusion.50) | copy-start | bytes 393220
  1235.9 266.7 %copy-start.42 = (bf16[512,1536]{1,0:T(8,128)(2,1)S(1)}, bf16[512,1536]{1,0:T(8,128)(2,1)}, u32[]{:S(2)}) copy-start(bf16[512,1536]{1,0:T(8,128)(2,1)} %gather_fusion.2) | copy-start | bytes 4718596
  1550.1 25.8 copy-start.25
  1722.8 22.1 copy-start.60
  1727.5 22.2 slice-start.7
  1975.4 794.9 %all-gather.45.cloned.1.call-start = ((), (), s32[]{:S(2)}) async-start(), calls=%async_computation.12 | async-start | bytes 15728640 | tf_op jit(solution)/shard_map/all_gather | solution.py:306
  1992.8 996.1 %all-gather.49.cloned.1.call-start = ((), (), s32[]{:S(2)}) async-start(), calls=%async_computation.14 | async-start | bytes 15728640 | tf_op jit(solution)/shard_map/all_gather | solution.py:307
  (177 other events, 1174.7 us)
Sparse Core Ops, SparseCore 0:
  9.6 143.8 all-gather.20
  155.0 150.7 all-gather.22
  307.4 26.5 all-gather.24
  335.4 27.4 all-gather.26
  364.3 114.8 all-gather.28
  480.6 113.5 all-gather.30
  595.7 113.5 all-gather.46
  710.9 242.1 all-gather.36
  954.7 242.1 all-gather.32
  1198.2 28.6 all-gather.38
  1228.5 29.5 all-gather.34
  1259.5 243.0 all-gather.40
  1504.1 28.6 all-gather.42
  1975.5 572.2 all-reduce.95
  2550.8 219.4 all-gather.44
  2772.4 216.3 all-gather.48
where the time goes:
time: 3020 us; the launch traced here: 3010 us
  waiting for transfers between devices  1740 us (58%)
  local copies, waits for them, and re-layouts  543 us (18%)
  blocking collectives  294 us (10%)
  matrix products  234 us (8%)
  other arithmetic  177 us (6%)
    psum x1, waiting for transfers between devices, local(): lax.psum((grad_down_branch, grad_up_branch, grad_down_gelu, grad_up_gelu,...  528 us
    pad x70, local copies, waits for them, and re-layouts, recurrence(): unused, state = lax.associative_scan(combine, (carried, driven), axis=0)  244 us
    all_gather x1, waiting for transfers between devices, local(): lax.all_gather(feed_down, 'shard', axis=0, tiled=True)  234 us
    all_gather x1, waiting for transfers between devices, local(): lax.all_gather(feed_up, 'shard', axis=1, tiled=True)  233 us
    all_gather x1, waiting for transfers between devices, local(): lax.all_gather(feed_gate, 'shard', axis=1, tiled=True)  231 us
    all_gather x1, waiting for transfers between devices, local(): lax.all_gather(grad_work, 'shard', axis=0, tiled=True)  210 us
    all_gather x1, waiting for transfers between devices, local(): lax.all_gather(work_out, 'shard', axis=0, tiled=True)  207 us
    slice x69, local copies, waits for them, and re-layouts, recurrence(): unused, state = lax.associative_scan(combine, (carried, driven), axis=0)  178 us
  transfers between devices with their start and end apart: 16, of which 11 were waited for; matrix products, arithmetic and copies ran while one was open for 16% of the time, Pallas kernels for 0%

commit v1 on v0

--- a/solution.py
+++ b/solution.py
@@ -315,7 +315,7 @@
     layer_out = jnp.take(collected[0], my_rows, axis=0)
     grad_tokens = jnp.take(collected[1], my_rows, axis=0)
     part_width = grad_down_branch.shape[1] // shards
-    summed = lax.psum(
+    one_axis = lax.psum(
         (
             grad_down_branch,
             grad_up_branch,
@@ -332,8 +332,9 @@
             grad_down_fdown,
             grad_up_fdown,
         ),
-        ("rep", "shard"),
-    )
+        "shard",
+    )
+    summed = lax.psum(one_axis, "rep")
     owned = tuple(
         (
             lax.dynamic_slice_in_dim(

time: 3020 us -> 3310 us (1.096)
  waiting for transfers between devices: 1740 us -> 2030 us
    psum x0 -> x1, waiting for transfers between devices: none -> 229 us  [local(): summed = lax.psum(one_axis, 'rep')]
    psum x1, waiting for transfers between devices: 528 us -> 581 us  [local(): lax.psum((grad_down_branch, grad_up_branch, grad_down_gelu, grad_up_gelu,...]
  transfers between devices with their start and end apart: 16 -> 17, of which waited for: 11 -> 12; matrix products, arithmetic and copies ran while one was open for 16% -> 15% of each run, Pallas kernels for 0% -> 0%
where the time goes in v1:
time: 3310 us; the launch traced here: 3300 us
  waiting for transfers between devices  2030 us (61%)
  local copies, waits for them, and re-layouts  544 us (16%)
  blocking collectives  295 us (9%)
  matrix products  234 us (7%)
  other arithmetic  177 us (5%)
    psum x1, waiting for transfers between devices, local(): lax.psum((grad_down_branch, grad_up_branch, grad_down_gelu, grad_up_gelu,...  581 us
    pad x70, local copies, waits for them, and re-layouts, recurrence(): unused, state = lax.associative_scan(combine, (carried, driven), axis=0)  244 us
    all_gather x1, waiting for transfers between devices, local(): lax.all_gather(feed_down, 'shard', axis=0, tiled=True)  234 us
    all_gather x1, waiting for transfers between devices, local(): lax.all_gather(feed_up, 'shard', axis=1, tiled=True)  233 us
    all_gather x1, waiting for transfers between devices, local(): lax.all_gather(feed_gate, 'shard', axis=1, tiled=True)  231 us
    psum x1, waiting for transfers between devices, local(): summed = lax.psum(one_axis, 'rep')  229 us
    all_gather x1, waiting for transfers between devices, local(): lax.all_gather(grad_work, 'shard', axis=0, tiled=True)  210 us
    all_gather x1, waiting for transfers between devices, local(): lax.all_gather(work_out, 'shard', axis=0, tiled=True)  210 us
  transfers between devices with their start and end apart: 17, of which 12 were waited for; matrix products, arithmetic and copies ran while one was open for 15% of the time, Pallas kernels for 0%

profile of v1, /device:TPU:0, one launch (start us, length us, event | category | flops | bytes accessed | tf_op | source)
XLA Modules:
  0.0 3295.3 jit_solution(15167056796754497916)
XLA Ops:
  19.0 15.8 all-gather.1
  35.1 17.6 all_gather.98
  52.7 23.2 all_gather.99
  76.7 16.9 all_gather.95
  93.7 14.5 all-gather
  108.3 20.1 all_gather.102
  128.4 17.1 all-gather.2
  145.5 11.9 all-gather.3
  158.1 21.5 all_gather.106
  179.5 21.5 all_gather.107
  201.0 22.2 all_gather.109
  223.2 22.3 all_gather.110
  245.5 11.9 all-gather.4
  258.0 21.2 all_gather.116
  279.2 22.0 all_gather.113
  301.2 15.2 all_gather.120
  348.1 9.0 copy.113
  362.8 8.3 add_add_fusion
  371.0 9.3 copy.142
  398.1 11.7 exponential_select_fusion
  409.8 9.8 slice.325
  419.6 9.8 slice.326
  429.4 9.8 slice.324
  439.2 9.8 slice.328
  556.3 10.1 slice.323
  566.4 10.1 slice.388
  598.7 8.7 pad.364
  616.2 16.5 pad.367
  638.7 16.5 pad.366
  678.3 30.9 all-gather.47.cloned.1.call-done
  719.9 233.1 %all-gather.37.cloned.1.call-done = bf16[1536,4608]{1,0:T(8,128)(2,1)} async-done(((bf16[1536,1152]{1,0:T(8,128)(2,1)}), bf16[1536,4608]{1,0:T(8,128)(2,1)}) %all-gather.37.cloned.1.call-update) | async-done | bytes 14155792 | tf_op jit(solution)/shard_map/all_gather | solution.py:231
  953.0 12.9 fusion.130
  965.9 230.8 %all-gather.33.cloned.1.call-done = bf16[1536,4608]{1,0:T(8,128)(2,1)} async-done(((bf16[1536,1152]{1,0:T(8,128)(2,1)}), bf16[1536,4608]{1,0:T(8,128)(2,1)}) %all-gather.33.cloned.1.call-update) | async-done | bytes 14155792 | tf_op jit(solution)/shard_map/all_gather | solution.py:230
  1196.7 12.9 fusion.129
  1209.6 17.2 all-gather.39.cloned.1.call-done
  1226.8 9.0 convolution_add_fusion.1
  1235.8 22.2 all-gather.35.cloned.1.call-done
  1258.0 10.0 convolution_add_fusion.2
  1268.0 234.5 %all-gather.41.cloned.1.call-done = bf16[4608,1536]{1,0:T(8,128)(2,1)} async-done(((bf16[1152,1536]{1,0:T(8,128)(2,1)}), bf16[4608,1536]{1,0:T(8,128)(2,1)}) %all-gather.41.cloned.1.call-update) | async-done | bytes 14155792 | tf_op jit(solution)/shard_map/all_gather | solution.py:232
  1502.5 13.3 fusion.95
  1515.8 16.9 all-gather.43.cloned.1.call-done
  1532.7 17.3 multiply_convert_fusion
  1550.0 13.4 fusion.131
  1564.8 10.3 convolution_add_fusion.12
  1598.3 9.8 slice.389
  1615.1 9.8 slice.390
  1714.0 8.7 pad.425
  1727.6 8.6 pad.450
  1736.2 8.8 pad.375
  1749.8 11.2 multiply_add_fusion.1
  1764.0 16.6 pad.426
  1780.6 16.5 pad.427
  1797.1 16.5 pad.451
  1813.6 16.6 pad.452
  1830.2 16.9 pad.370
  1847.1 16.9 pad.428
  1864.0 18.4 multiply_multiply_fusion.5
  1977.1 12.4 convolution_add_fusion.13
  2011.1 581.3 %all-reduce.100.cloned.1.call-done = (f32[1536,128]{0,1:T(8,128)}, f32[128,2048]{1,0:T(8,128)}, f32[1536,128]{0,1:T(8,128)}, f32[128,2048]{1,0:T(8,128)}, f32[20...) async-done(((f32[1536,128]{0,1:T(8,128)}, ...) | async-done | bytes 18087952 | tf_op jit(solution)/shard_map/psum | solution.py:318
  2601.3 209.5 %all-gather.45.cloned.1.call-done = f32[2048,1536]{1,0:T(8,128)} async-done(((f32[512,1536]{1,0:T(8,128)}), f32[2048,1536]{1,0:T(8,128)}) %all-gather.45.cloned.1.call-update) | async-done | bytes 12582928 | tf_op jit(solution)/shard_map/all_gather | solution.py:306
  2810.9 8.3 gather_fusion.1
  2819.1 210.2 %all-gather.49.cloned.1.call-done = f32[2048,1536]{1,0:T(8,128)} async-done(((f32[512,1536]{1,0:T(8,128)}), f32[2048,1536]{1,0:T(8,128)}) %all-gather.49.cloned.1.call-update) | async-done | bytes 12582928 | tf_op jit(solution)/shard_map/all_gather | solution.py:307
  3029.4 9.1 gather_fusion.3
  3043.9 229.5 %all-reduce.98.cloned.1.call-done = (f32[1536,128]{0,1:T(8,128)}, f32[128,2048]{1,0:T(8,128)}, f32[1536,128]{0,1:T(8,128)}, f32[128,2048]{1,0:T(8,128)}, f32[204...) async-done(((f32[1536,128]{0,1:T(8,128)}, ...) | async-done | bytes 18087952 | tf_op jit(solution)/shard_map/psum | solution.py:337
  (800 shorter events, 522.9 us)
Async XLA Ops:
  7.2 311.2 %all-gather.21.cloned.1.call-start = ((), (), s32[]{:S(2)}) async-start(), calls=%async_computation | async-start | bytes 7864320 | tf_op jit(solution)/shard_map/all_gather | solution.py:126
  7.9 321.5 %all-gather.23.cloned.1.call-start = ((), (), s32[]{:S(2)}) async-start(), calls=%async_computation.1 | async-start | bytes 7864320 | tf_op jit(solution)/shard_map/all_gather | solution.py:134
  8.7 332.8 %all-gather.25.cloned.1.call-start = ((), (), s32[]{:S(2)}) async-start(), calls=%async_computation.2 | async-start | bytes 1310720 | tf_op jit(solution)/shard_map/all_gather | solution.py:138
  9.4 353.3 %all-gather.27.cloned.1.call-start = ((), (), s32[]{:S(2)}) async-start(), calls=%async_computation.3 | async-start | bytes 1310720 | tf_op jit(solution)/shard_map/all_gather | solution.py:160
  10.0 645.9 %all-gather.29.cloned.1.call-start = ((), (), s32[]{:S(2)}) async-start(), calls=%async_computation.4 | async-start | bytes 7864320 | tf_op jit(solution)/shard_map/all_gather | solution.py:135
  10.6 657.5 %all-gather.31.cloned.1.call-start = ((), (), s32[]{:S(2)}) async-start(), calls=%async_computation.5 | async-start | bytes 7864320 | tf_op jit(solution)/shard_map/all_gather | solution.py:141
  11.1 698.1 %all-gather.47.cloned.1.call-start = ((), (), s32[]{:S(2)}) async-start(), calls=%async_computation.13 | async-start | bytes 7864320 | tf_op jit(solution)/shard_map/all_gather | solution.py:127
  11.9 941.1 %all-gather.37.cloned.1.call-start = ((), (), s32[]{:S(2)}) async-start(), calls=%async_computation.8 | async-start | bytes 17694720 | tf_op jit(solution)/shard_map/all_gather | solution.py:231
  12.7 22.2 copy-start.211
  12.7 22.4 copy-start.168
  12.7 40.1 %copy-start.157 = (bf16[32,2048]{1,0:T(8,128)(2,1)S(1)}, bf16[32,2048]{1,0:T(8,128)(2,1)}, u32[]{:S(2)}) copy-start(bf16[32,2048]{1,0:T(8,128)(2,1)} %param.52) | copy-start | bytes 393220
  12.7 64.0 %copy-start.204 = (bf16[4,512]{1,0:T(4,128)(2,1)S(1)}, bf16[4,512]{1,0:T(4,128)(2,1)}, u32[]{:S(2)}) copy-start(bf16[4,512]{1,0:T(4,128)(2,1)} %param.41) | copy-start | bytes 12292
  12.7 81.0 %copy-start.206 = (bf16[512]{0:T(512)(128)(2,1)S(1)}, bf16[512]{0:T(512)(128)(2,1)}, u32[]{:S(2)}) copy-start(bf16[512]{0:T(512)(128)(2,1)} %param.42) | copy-start | bytes 3076
  12.7 1184.0 %all-gather.33.cloned.1.call-start = ((), (), s32[]{:S(2)}) async-start(), calls=%async_computation.6 | async-start | bytes 17694720 | tf_op jit(solution)/shard_map/all_gather | solution.py:230
  13.4 94.8 %copy-start.158 = (bf16[2048,32]{0,1:T(8,128)(2,1)S(1)}, bf16[2048,32]{0,1:T(8,128)(2,1)}, u32[]{:S(2)}) copy-start(bf16[2048,32]{0,1:T(8,128)(2,1)} %param.55) | copy-start | bytes 393220
  13.5 114.9 %copy-start.205 = (bf16[4,256]{1,0:T(4,128)(2,1)S(1)}, bf16[4,256]{1,0:T(4,128)(2,1)}, u32[]{:S(2)}) copy-start(bf16[4,256]{1,0:T(4,128)(2,1)} %param.44) | copy-start | bytes 6148
  13.5 132.0 %copy-start.207 = (bf16[512]{0:T(512)(128)(2,1)S(1)}, bf16[512]{0:T(512)(128)(2,1)}, u32[]{:S(2)}) copy-start(bf16[512]{0:T(512)(128)(2,1)} %param.45) | copy-start | bytes 3076
  13.5 144.6 %copy-start.169 = (bf16[1536,32]{0,1:T(8,128)(2,1)S(1)}, bf16[1536,32]{0,1:T(8,128)(2,1)}, u32[]{:S(2)}) copy-start(bf16[1536,32]{0,1:T(8,128)(2,1)} %param.53) | copy-start | bytes 294916
  13.5 166.0 %copy-start.159 = (bf16[32,2048]{1,0:T(8,128)(2,1)S(1)}, bf16[32,2048]{1,0:T(8,128)(2,1)}, u32[]{:S(2)}) copy-start(bf16[32,2048]{1,0:T(8,128)(2,1)} %param.54) | copy-start | bytes 393220
  13.5 1213.3 %all-gather.39.cloned.1.call-start = ((), (), s32[]{:S(2)}) async-start(), calls=%async_computation.9 | async-start | bytes 1474560 | tf_op jit(solution)/shard_map/all_gather | solution.py:166
  14.1 186.9 %copy-start.160 = (bf16[2048,32]{0,1:T(8,128)(2,1)S(1)}, bf16[2048,32]{0,1:T(8,128)(2,1)}, u32[]{:S(2)}) copy-start(bf16[2048,32]{0,1:T(8,128)(2,1)} %param.57) | copy-start | bytes 393220
  14.1 1243.9 %all-gather.35.cloned.1.call-start = ((), (), s32[]{:S(2)}) async-start(), calls=%async_computation.7 | async-start | bytes 1474560 | tf_op jit(solution)/shard_map/all_gather | solution.py:164
  14.8 208.4 %copy-start.170 = (bf16[32,1536]{1,0:T(8,128)(2,1)S(1)}, bf16[32,1536]{1,0:T(8,128)(2,1)}, u32[]{:S(2)}) copy-start(bf16[32,1536]{1,0:T(8,128)(2,1)} %param.58) | copy-start | bytes 294916
  14.8 230.7 %copy-start.209 = (bf16[384]{0:T(512)(128)(2,1)S(1)}, bf16[384]{0:T(512)(128)(2,1)}, u32[]{:S(2)}) copy-start(bf16[384]{0:T(512)(128)(2,1)} %param.47) | copy-start | bytes 2308
  14.9 243.2 %copy-start.171 = (bf16[1536,32]{0,1:T(8,128)(2,1)S(1)}, bf16[1536,32]{0,1:T(8,128)(2,1)}, u32[]{:S(2)}) copy-start(bf16[1536,32]{0,1:T(8,128)(2,1)} %param.61) | copy-start | bytes 294916
  14.9 264.4 %copy-start.172 = (bf16[1536,32]{0,1:T(8,128)(2,1)S(1)}, bf16[1536,32]{0,1:T(8,128)(2,1)}, u32[]{:S(2)}) copy-start(bf16[1536,32]{0,1:T(8,128)(2,1)} %param.59) | copy-start | bytes 294916
  14.9 286.4 %copy-start.173 = (bf16[32,1536]{1,0:T(8,128)(2,1)S(1)}, bf16[32,1536]{1,0:T(8,128)(2,1)}, u32[]{:S(2)}) copy-start(bf16[32,1536]{1,0:T(8,128)(2,1)} %param.64) | copy-start | bytes 294916
  14.9 1487.6 %all-gather.41.cloned.1.call-start = ((), (), s32[]{:S(2)}) async-start(), calls=%async_computation.10 | async-start | bytes 17694720 | tf_op jit(solution)/shard_map/all_gather | solution.py:232
  15.5 1517.2 %all-gather.43.cloned.1.call-start = ((), (), s32[]{:S(2)}) async-start(), calls=%async_computation.11 | async-start | bytes 1474560 | tf_op jit(solution)/shard_map/all_gather | solution.py:167
  16.2 2576.2 %all-reduce.100.cloned.1.call-start = ((), (), s32[]{:S(2)}) async-start(), calls=%async_computation.16 | async-start | bytes 36175872 | tf_op jit(solution)/shard_map/psum | solution.py:318
  34.8 292.0 %copy-start.177 = (f32[1536]{0:T(1024)}, f32[1536]{0:T(1024)S(1)}, u32[]{:S(2)}) copy-start(f32[1536]{0:T(1024)S(1)} %reshape.246) | copy-start | bytes 18436
  52.7 276.1 %copy-start.72 = (bf16[1536,128]{0,1:T(8,128)(2,1)}, bf16[1536,128]{0,1:T(8,128)(2,1)S(1)}, u32[]{:S(2)}) copy-start(bf16[1536,128]{0,1:T(8,128)(2,1)S(1)} %all_gather.98) | copy-start | bytes 1179652
  75.9 259.1 %copy-start.49 = (bf16[128,2048]{1,0:T(8,128)(2,1)}, bf16[128,2048]{1,0:T(8,128)(2,1)S(1)}, u32[]{:S(2)}) copy-start(bf16[128,2048]{1,0:T(8,128)(2,1)S(1)} %all_gather.99) | copy-start | bytes 1572868
  76.7 321.4 %copy-start.198 = (pred[512]{0:T(512)(128)(4,1)}, pred[512]{0:T(512)(128)(4,1)S(1)}, u32[]{:S(2)}) copy-start(pred[512]{0:T(512)(128)(4,1)S(1)} %get-tuple-element.160) | copy-start | bytes 1540
  93.7 242.1 %copy-start.175 = (f32[1,2048]{1,0:T(1,128)}, f32[1,2048]{1,0:T(1,128)S(1)}, u32[]{:S(2)}) copy-start(f32[1,2048]{1,0:T(1,128)S(1)} %get-tuple-element.154) | copy-start | bytes 24580
  93.7 242.1 %copy-start.179 = (f32[1,2048]{1,0:T(1,128)}, f32[1,2048]{1,0:T(1,128)S(1)}, u32[]{:S(2)}) copy-start(f32[1,2048]{1,0:T(1,128)S(1)} %get-tuple-element.155) | copy-start | bytes 24580
  93.7 242.1 %copy-start.181 = (f32[1,2048]{1,0:T(1,128)}, f32[1,2048]{1,0:T(1,128)S(1)}, u32[]{:S(2)}) copy-start(f32[1,2048]{1,0:T(1,128)S(1)} %get-tuple-element.157) | copy-start | bytes 24580
  93.7 242.1 %copy-start.183 = (f32[1,2048]{1,0:T(1,128)}, f32[1,2048]{1,0:T(1,128)S(1)}, u32[]{:S(2)}) copy-start(f32[1,2048]{1,0:T(1,128)S(1)} %get-tuple-element.156) | copy-start | bytes 24580
  128.4 228.7 %copy-start.46 = (bf16[2048,128]{0,1:T(8,128)(2,1)}, bf16[2048,128]{0,1:T(8,128)(2,1)S(1)}, u32[]{:S(2)}) copy-start(bf16[2048,128]{0,1:T(8,128)(2,1)S(1)} %all_gather.102) | copy-start | bytes 1572868
  158.1 240.0 %copy-start.151 = (f32[2048]{0:T(1024)}, f32[2048]{0:T(1024)S(1)}, u32[]{:S(2)}) copy-start(f32[2048]{0:T(1024)S(1)} %get-tuple-element.159) | copy-start | bytes 24580
  328.8 327.0 %copy-start.12 = (bf16[512,1536]{1,0:T(8,128)(2,1)}, bf16[512,1536]{1,0:T(8,128)(2,1)S(1)}, u32[]{:S(2)}) copy-start(bf16[512,1536]{1,0:T(8,128)(2,1)S(1)} %fusion.33) | copy-start | bytes 4718596
  497.7 41.7 %copy-start.62 = (f32[32,2048]{1,0:T(8,128)}, f32[32,2048]{1,0:T(8,128)S(1)}, u32[]{:S(2)}) copy-start(f32[32,2048]{1,0:T(8,128)S(1)} %slice.342) | copy-start | bytes 786436
  501.5 33.2 %copy-start.76 = (f32[64,2048]{1,0:T(8,128)S(1)}, f32[64,2048]{1,0:T(8,128)}, u32[]{:S(2)}) copy-start(f32[64,2048]{1,0:T(8,128)} %get-tuple-element.109) | copy-start | bytes 1572868
  502.5 47.2 %copy-start.111 = (f32[16,2048]{1,0:T(8,128)}, f32[16,2048]{1,0:T(8,128)S(1)}, u32[]{:S(2)}) copy-start(f32[16,2048]{1,0:T(8,128)S(1)} %slice.349) | copy-start | bytes 393220
  505.2 44.6 %copy-start.88 = (f32[16,2048]{1,0:T(8,128)}, f32[16,2048]{1,0:T(8,128)S(1)}, u32[]{:S(2)}) copy-start(f32[16,2048]{1,0:T(8,128)S(1)} %slice.348) | copy-start | bytes 393220
  506.2 43.5 %copy-start.113 = (f32[16,2048]{1,0:T(8,128)}, f32[16,2048]{1,0:T(8,128)S(1)}, u32[]{:S(2)}) copy-start(f32[16,2048]{1,0:T(8,128)S(1)} %slice.352) | copy-start | bytes 393220
  507.3 24.8 copy-start.130
  508.0 47.4 %copy-start.126 = (f32[8,2048]{1,0:T(8,128)}, f32[8,2048]{1,0:T(8,128)S(1)}, u32[]{:S(2)}) copy-start(f32[8,2048]{1,0:T(8,128)S(1)} %slice.354) | copy-start | bytes 196612
  508.0 24.1 copy-start.132
  521.6 33.7 %copy-start.162 = (f32[1,2048]{1,0:T(1,128)}, f32[1,2048]{1,0:T(1,128)S(1)}, u32[]{:S(2)}) copy-start(f32[1,2048]{1,0:T(1,128)S(1)} %get-tuple-element.152) | copy-start | bytes 24580
  528.1 50.0 %copy-start.128 = (f32[7,2048]{1,0:T(8,128)}, f32[7,2048]{1,0:T(8,128)S(1)}, u32[]{:S(2)}) copy-start(f32[7,2048]{1,0:T(8,128)S(1)} %slice.353) | copy-start | bytes 172036
  530.4 48.5 %copy-start.109 = (f32[15,2048]{1,0:T(8,128)}, f32[15,2048]{1,0:T(8,128)S(1)}, u32[]{:S(2)}) copy-start(f32[15,2048]{1,0:T(8,128)S(1)} %slice.347) | copy-start | bytes 368644
  534.7 45.7 %copy-start.77 = (f32[31,2048]{1,0:T(8,128)}, f32[31,2048]{1,0:T(8,128)S(1)}, u32[]{:S(2)}) copy-start(f32[31,2048]{1,0:T(8,128)S(1)} %slice.341) | copy-start | bytes 761860
  677.1 519.6 %copy-start.14 = (bf16[512,1536]{1,0:T(8,128)(2,1)}, bf16[512,1536]{1,0:T(8,128)(2,1)S(1)}, u32[]{:S(2)}) copy-start(bf16[512,1536]{1,0:T(8,128)(2,1)S(1)} %multiply_convert_fusion.3) | copy-start | bytes 4718596
  677.7 549.1 %copy-start.92 = (bf16[512,128]{1,0:T(8,128)(2,1)}, bf16[512,128]{1,0:T(8,128)(2,1)S(1)}, u32[]{:S(2)}) copy-start(bf16[512,128]{1,0:T(8,128)(2,1)S(1)} %fusion.49) | copy-start | bytes 393220
  678.3 579.7 %copy-start.94 = (bf16[512,128]{1,0:T(8,128)(2,1)}, bf16[512,128]{1,0:T(8,128)(2,1)S(1)}, u32[]{:S(2)}) copy-start(bf16[512,128]{1,0:T(8,128)(2,1)S(1)} %fusion.48) | copy-start | bytes 393220
  719.9 812.8 %copy-start.155 = (bf16[512,128]{1,0:T(8,128)(2,1)}, bf16[512,128]{1,0:T(8,128)(2,1)S(1)}, u32[]{:S(2)}) copy-start(bf16[512,128]{1,0:T(8,128)(2,1)S(1)} %fusion.50) | copy-start | bytes 393220
  1235.8 266.7 %copy-start.42 = (bf16[512,1536]{1,0:T(8,128)(2,1)S(1)}, bf16[512,1536]{1,0:T(8,128)(2,1)}, u32[]{:S(2)}) copy-start(bf16[512,1536]{1,0:T(8,128)(2,1)} %gather_fusion.2) | copy-start | bytes 4718596
  1550.0 25.8 copy-start.25
  1722.8 22.2 copy-start.60
  1727.6 22.3 slice-start.7
  1975.2 835.6 %all-gather.45.cloned.1.call-start = ((), (), s32[]{:S(2)}) async-start(), calls=%async_computation.12 | async-start | bytes 15728640 | tf_op jit(solution)/shard_map/all_gather | solution.py:306
  1992.6 1036.8 %all-gather.49.cloned.1.call-start = ((), (), s32[]{:S(2)}) async-start(), calls=%async_computation.14 | async-start | bytes 15728640 | tf_op jit(solution)/shard_map/all_gather | solution.py:307
  2011.1 1262.2 %all-reduce.98.cloned.1.call-start = ((), (), s32[]{:S(2)}) async-start(), calls=%async_computation.15 | async-start | bytes 36175872 | tf_op jit(solution)/shard_map/psum | solution.py:337
  (178 other events, 1192.4 us)
Sparse Core Ops, SparseCore 0:
  9.6 143.6 all-gather.20
  154.8 151.5 all-gather.22
  308.0 25.8 all-gather.24
  335.3 27.4 all-gather.26
  364.2 114.8 all-gather.28
  480.5 113.5 all-gather.30
  595.6 113.5 all-gather.46
  710.8 242.1 all-gather.36
  954.6 242.1 all-gather.32
  1198.1 28.6 all-gather.38
  1228.4 29.5 all-gather.34
  1259.4 243.0 all-gather.40
  1504.0 28.6 all-gather.42
  1975.3 617.0 all-reduce.99
  2594.0 216.8 all-gather.44
  2812.9 216.3 all-gather.48
  3036.8 236.5 all-reduce.97
